TPU v7x, 32 devices: a whole 2x2x4 slice. The times are simulated.
32 devices in a mesh: ex: 8 (over z, y), ckpt: 4 (over x, core).
Axes of the slice: x: 2, y: 2, z: 4, core: 2. Of those that a mesh axis runs over, the one named last changes fastest.
Arguments:
- grads: bfloat16 [4, 2560, 4096], P('ckpt', 'ex'), may hold values from -6 to 6
- second_moment: float32 [4, 4096], P('ckpt'), may hold values from 0.25 to 4
- step_size: float32 [4], P('ckpt'), may hold values from 0.25 to 1
- partners: int32 [8, 2], P('ex'), may hold values from -1 to 7, as said below
- counts: int32 [8], P('ex'), may hold values from 1 to 2, as said below
Outputs:
- band_rows: float32 [2560, 1280], P('ex', 'ckpt')
Inputs may be any that keep to these rules, and one draw needn't show every extreme that they name: For s < counts[b], partners[b, s] are distinct blocks among (b + 1) mod 8 to (b + 2) mod 8; slots from counts[b] on hold -1. `counts`: some block has 2 live slots in every draw.
All inputs are finite; a program needn't handle non-finite values.
Results may differ from a plain program's by a relative error of at most 0.0029.
Values may be sent and summed in bfloat16 or wider, within the bound.
A program may use at most 64 MiB of HBM per device.

v0:
```python
import jax
import jax.numpy as jnp
from jax import lax
from jax.sharding import PartitionSpec as P

EPSILON = 1e-08


def passed_along(value, axis, by):
    length = lax.axis_size(axis)
    return lax.ppermute(value, axis, [(i, (i + by) % length) for i in range(length)])


def local(grads, second_moment, step_size, partners, counts):
    width = grads.shape[2]
    block_rows = grads.shape[1]
    reach = partners.shape[1]
    blocks = lax.axis_size("ex")
    position = lax.axis_index("ex")
    factor = step_size[:, None] / (jnp.sqrt(second_moment) + EPSILON) * width ** (-0.5)
    scaled = (grads.astype(jnp.float32) * factor[:, None, :]).astype(jnp.bfloat16)
    offsets = jnp.mod(partners[0] - position, blocks)
    alive_slot = jnp.arange(reach, dtype=jnp.int32) < counts[0]
    wanted = jnp.arange(1, reach + 1, dtype=jnp.int32)
    matched = jnp.logical_and(offsets[:, None] == wanted[None, :], alive_slot[:, None])
    listed = jnp.sum(matched.astype(jnp.float32), axis=0)
    forward_list = []
    for offset in range(1, reach + 1):
        visitor = passed_along(grads, "ex", -offset)
        forward_list.append(
            lax.dot_general(
                scaled, visitor, (((0, 2), (0, 2)), ((), ())), preferred_element_type=jnp.float32
            )
            * listed[offset - 1]
        )
    stacked = jnp.stack(forward_list, axis=1)
    returned = []
    for offset in range(reach, 0, -1):
        arrived = passed_along(stacked[:, offset - 1, :], "ex", offset)
        returned.append(arrived.T)
    panel = jnp.concatenate([jnp.stack(returned, axis=1), stacked], axis=1)
    panel = panel.reshape(block_rows, 2 * reach * block_rows)
    return lax.psum_scatter(panel, "ckpt", scatter_dimension=1, tiled=True)


def solution(mesh):
    in_specs = (P("ckpt", "ex", None), P("ckpt", None), P("ckpt"), P("ex", None), P("ex"))
    out_specs = P("ex", "ckpt")
    return jax.shard_map(local, mesh=mesh, in_specs=in_specs, out_specs=out_specs, check_vma=False)
```

profile of v0, /device:TPU:0, one launch (start us, length us, event | category | flops | bytes accessed | tf_op | source)
XLA Modules:
  0.0 183.3 jit_solution(9039904103414942351)
XLA Ops:
  6.5 0.0 reduce-scatter.4.cloned.1.call-start
  6.5 6.0 %collective-permute-start.2 = (bf16[1,320,4096]{2,1,0:T(8,128)(2,1)}, bf16[1,320,4096]{2,1,0:T(8,128)(2,1)S(1)}, u32[]{:S(2)}, u32[]{:S(2)}) collective-permute-start(bf16[1,320,4096]{2,1,0:T(8,128)(2,1)} %param.5), channel_id=1, source_target_pairs={{0,28},{4,0},{8,4},{12,8},{16,12},{20,16},{24,20},{28,24},{1,29},{... | collective-permute-start | bytes 7864328 | tf_op jit(solution)/shard_map/ppermute | solution.py:11
  12.6 0.4 collective-permute-start
  14.3 0.7 and_select_fusion
  15.0 0.1 fusion.17
  15.1 0.7 fusion.19
  15.8 0.8 divide_multiply_fusion
  16.5 53.6 %collective-permute-done.2 = bf16[1,320,4096]{2,1,0:T(8,128)(2,1)S(1)} collective-permute-done((bf16[1,320,4096]{2,1,0:T(8,128)(2,1)}, bf16[1,320,4096]{2,1,0:T(8,128)(2,1)S(1)}, u32[]{:S(2)}, u32[]{:S(2)}) %collective-permute-start.2) | collective-permute-done | bytes 2621472 | tf_op jit(solution)/shard_map/ppermute | solution.py:11
  70.1 0.0 copy-start
  70.1 4.1 %fusion.12 = f32[320,320]{0,1:T(8,128)S(1)} fusion(bf16[1,320,4096]{2,1,0:T(8,128)(2,1)S(1)} %collective-permute-done.2, bf16[1,320,4096]{2,1,0:T(8,128)(2,1)} %param.5, f32[4096]{0:T(1024)S(1)} %bitcast.45, f32[]{:T(128)} %bitcast.10), kind=kOutput, calls=%fused_computation.8 | convolution fusion | flops 842895360 | bytes 5668868 | tf_op jit(solution)/shard_map/dot_general | solution.py:31
  74.2 0.3 collective-permute-start.3
  74.5 50.7 %collective-permute-done = bf16[1,320,4096]{2,1,0:T(8,128)(2,1)} collective-permute-done((bf16[1,320,4096]{2,1,0:T(8,128)(2,1)}, bf16[1,320,4096]{2,1,0:T(8,128)(2,1)}, u32[]{:S(2)}, u32[]{:S(2)}) %collective-permute-start) | collective-permute-done | bytes 2621472 | tf_op jit(solution)/shard_map/ppermute | solution.py:11
  125.2 0.0 copy-done
  125.2 4.0 %fusion.7 = f32[320,320]{0,1:T(8,128)S(1)} fusion(bf16[1,320,4096]{2,1,0:T(8,128)(2,1)} %collective-permute-done, bf16[1,320,4096]{2,1,0:T(8,128)(2,1)S(1)} %copy-done, f32[4096]{0:T(1024)S(1)} %bitcast.46, f32[]{:T(128)} %bitcast.6), kind=kOutput, calls=%fused_computation.7 | convolution fusion | flops 842895360 | bytes 5668868 | tf_op jit(solution)/shard_map/dot_general | solution.py:31
  129.2 0.2 copy.12
  129.4 0.5 collective-permute-start.1
  129.9 0.0 collective-permute-done.3
  129.9 0.2 copy.13
  130.1 14.0 %collective-permute-done.1 = f32[320,320]{1,0:T(8,128)S(1)} collective-permute-done((f32[320,320]{1,0:T(8,128)S(1)}, f32[320,320]{1,0:T(8,128)S(1)}, u32[]{:S(2)}, u32[]{:S(2)}) %collective-permute-start.1) | collective-permute-done | bytes 409632 | tf_op jit(solution)/shard_map/ppermute | solution.py:11
  144.1 1.4 pad_maximum_fusion
  145.5 0.0 reduce-scatter.4.cloned.1.call-update
  145.5 29.0 %reduce-scatter.4.cloned.1.call-done = f32[320,320]{1,0:T(8,128)} async-done(((f32[1280,320]{1,0:T(8,128)}), f32[320,320]{1,0:T(8,128)}) %reduce-scatter.4.cloned.1.call-update) | async-done | bytes 409616
  174.5 2.0 %copy.16 = f32[320,320]{1,0:T(8,128)} copy(f32[320,320]{0,1:T(8,128)} %bitcast.44) | data formatting | bytes 819200
  (1 shorter events, 0.0 us)
Async XLA Ops:
  6.5 167.9 %reduce-scatter.4.cloned.1.call-start = ((), (), s32[]{:S(2)}) async-start(), calls=%async_computation.1 | async-start | bytes 2457600
  6.5 63.6 %collective-permute-start.2 = (bf16[1,320,4096]{2,1,0:T(8,128)(2,1)}, bf16[1,320,4096]{2,1,0:T(8,128)(2,1)S(1)}, u32[]{:S(2)}, u32[]{:S(2)}) collective-permute-start(bf16[1,320,4096]{2,1,0:T(8,128)(2,1)} %param.5), channel_id=1, source_target_pairs={{0,28},{4,0},{8,4},{12,8},{16,12},{20,16},{24,20},{28,24},{1,29},{... | collective-permute-start | bytes 7864328 | tf_op jit(solution)/shard_map/ppermute | solution.py:11
  12.6 112.6 %collective-permute-start = (bf16[1,320,4096]{2,1,0:T(8,128)(2,1)}, bf16[1,320,4096]{2,1,0:T(8,128)(2,1)}, u32[]{:S(2)}, u32[]{:S(2)}) collective-permute-start(bf16[1,320,4096]{2,1,0:T(8,128)(2,1)} %param.5), channel_id=1, source_target_pairs={{0,24},{4,28},{8,0},{12,4},{16,8},{20,12},{24,16},{28,20},{1,25},{... | collective-permute-start | bytes 7864328 | tf_op jit(solution)/shard_map/ppermute | solution.py:11
  70.1 55.0 %copy-start = (bf16[1,320,4096]{2,1,0:T(8,128)(2,1)S(1)}, bf16[1,320,4096]{2,1,0:T(8,128)(2,1)}, u32[]{:S(2)}) copy-start(bf16[1,320,4096]{2,1,0:T(8,128)(2,1)} %param.5) | copy-start | bytes 7864324
  74.2 55.7 %collective-permute-start.3 = (f32[320,320]{0,1:T(8,128)S(1)}, f32[320,320]{0,1:T(8,128)S(1)}, u32[]{:S(2)}, u32[]{:S(2)}) collective-permute-start(f32[320,320]{0,1:T(8,128)S(1)} %fusion.12), channel_id=1, source_target_pairs={{0,4},{4,8},{8,12},{12,16},{16,20},{20,24},{24,28},{28,0},{1,5},{5... | collective-permute-start | bytes 1228808 | tf_op jit(solution)/shard_map/ppermute | solution.py:11
  129.4 14.7 %collective-permute-start.1 = (f32[320,320]{1,0:T(8,128)S(1)}, f32[320,320]{1,0:T(8,128)S(1)}, u32[]{:S(2)}, u32[]{:S(2)}) collective-permute-start(f32[320,320]{1,0:T(8,128)S(1)} %copy.12), channel_id=1, source_target_pairs={{0,8},{4,12},{8,16},{12,20},{16,24},{20,28},{24,0},{28,4},{1,9},{5... | collective-permute-start | bytes 1228808 | tf_op jit(solution)/shard_map/ppermute | solution.py:11
Sparse Core Ops, SparseCore 0:
  145.6 28.7 reduce-scatter.3
where the time goes:
time: 184 us; the launch traced here: 183 us
  waiting for transfers between devices  147 us (80%)
  between operations  14.7 us (8%)
  matrix products  8.03 us (4%)
  starting transfers between devices  7.27 us (4%)
  local copies, waits for them, and re-layouts  3.12 us (2%)
  other arithmetic  2.96 us (2%)
    ppermute x4, waiting for transfers between devices, passed_along(): lax.ppermute(value, axis, [(i, (i + by) % length) for i in range(length)])  118 us
    unnamed x2, waiting for transfers between devices  29 us
    dot_general x2, matrix products, local(): lax.dot_general(scaled, visitor, (((0, 2), (0, 2)), ((), ())), preferred_...  8.03 us
    ppermute x4, starting transfers between devices, passed_along(): lax.ppermute(value, axis, [(i, (i + by) % length) for i in range(length)])  7.27 us
  transfers between devices with their start and end apart: 5, of which 4 were waited for; matrix products, arithmetic and copies ran while one was open for 6% of the time, Pallas kernels for 0%

commit v1 on v0

--- a/solution.py
+++ b/solution.py
@@ -1,9 +1,15 @@
+import functools
+
 import jax
 import jax.numpy as jnp
 from jax import lax
+from jax.experimental import pallas as pl
+from jax.experimental.pallas import tpu as pltpu
 from jax.sharding import PartitionSpec as P
 
 EPSILON = 1e-08
+MESH = pl.DeviceIdType.MESH
+PIECES = 8
 
 
 def passed_along(value, axis, by):
@@ -11,7 +17,7 @@
     return lax.ppermute(value, axis, [(i, (i + by) % length) for i in range(length)])
 
 
-def local(grads, second_moment, step_size, partners, counts):
+def general(grads, second_moment, step_size, partners, counts):
     width = grads.shape[2]
     block_rows = grads.shape[1]
     reach = partners.shape[1]
@@ -43,6 +49,275 @@
     return lax.psum_scatter(panel, "ckpt", scatter_dimension=1, tiled=True)
 
 
+def kernel(
+    blocks, reach, g_ref, moment_ref, step_ref, partners_ref, counts_ref, out_ref,
+    own, oth, early, late, factor, acc, half, quarter, piece, half_in, quarter_in, parts,
+    flag_own, flag_in, turned,
+    own_sem, y_send, y_recv, e_send, e_recv, l_send, l_recv,
+    h_send, h_recv, q_send, q_recv, p_send, parts_recv, f_send, f_recv,
+):
+    rows, width = g_ref.shape
+    layers = blocks // 2
+    span = width // 2
+    piece_width = span // PIECES
+    half_rows, quarter_rows = rows // 2, rows // 4
+    e = lax.axis_index("ex")
+    c = lax.axis_index("ckpt")
+    z, y = e // 2, e % 2
+    core, x = c % 2, c // 2
+
+    mate = (2 * z + 1 - y, c)
+    ahead = ((e + 2 * (2 * y - 1) + blocks) % blocks, c)
+    behind = ((e - 2 * (2 * y - 1) + blocks) % blocks, c)
+    core_mate = (e, c + 1 - 2 * core)
+    x_mate = (e, (c + 2) % 4)
+    offset = 2 - ((c + 1) // 2) % 2
+    flag_to = ((e + offset) % blocks, c)
+    flag_from = ((e - offset + blocks) % blocks, c)
+
+    def owners(slot):
+        a, o = [(2 * z, 1), (2 * z - y, 2), (2 * z + 1 - 2 * y, 1), (2 * z - 1 + y, 2)][slot]
+        a = (a + blocks) % blocks
+        return (a, reach - 1 + o), ((a + o) % blocks, reach - o)
+
+    tile_row = (e - (1 - x) * offset + blocks) % blocks
+    odd = tile_row % 2
+    sources = []
+    for row in range(2):
+        layer = (tile_row // 2 + odd * ((offset - 1) + (2 - offset) * row)) % layers
+        sources += [(2 * layer + row, q) for q in range(4)]
+
+    barrier = pltpu.get_barrier_semaphore()
+
+    for device in [mate, ahead, behind, core_mate, x_mate, flag_from] + sources:
+        pl.semaphore_signal(barrier, inc=1, device_id=device, device_id_type=MESH)
+
+    mine = pl.multiple_of(y * span, 128)
+    theirs = pl.multiple_of((1 - y) * span, 128)
+    own_copies = [
+        pltpu.make_async_copy(
+            g_ref.at[:, pl.ds(mine + j * piece_width, piece_width)], own.at[j], own_sem.at[j]
+        )
+        for j in range(PIECES)
+    ]
+    for copy in own_copies:
+        copy.start()
+
+    total = jnp.float32(0)
+    for s in range(reach):
+        apart = (partners_ref[0, s] - e + blocks) % blocks
+        live = jnp.logical_and(apart == offset, s < counts_ref[0])
+        total = total + jnp.where(live, jnp.float32(1), jnp.float32(0))
+    flag_own[...] = jnp.full(flag_own.shape, total, jnp.float32)
+    scale = step_ref[0] / (jnp.sqrt(moment_ref[:, pl.ds(mine, span)]) + EPSILON) * width ** (-0.5)
+    for j in range(PIECES):
+        factor[j] = scale[:, j * piece_width : (j + 1) * piece_width]
+
+    pl.semaphore_wait(barrier, 14)
+
+    def remote(src, dst, send, recv, device):
+        return pltpu.make_async_remote_copy(
+            src_ref=src, dst_ref=dst, send_sem=send, recv_sem=recv, device_id=device, device_id_type=MESH
+        )
+
+    flag_copy = remote(flag_own, flag_in, f_send, f_recv, flag_to)
+    y_copies, e_copies, l_copies = [], [], []
+    for j in range(PIECES):
+        y_copies.append(
+            remote(
+                g_ref.at[:, pl.ds(theirs + j * piece_width, piece_width)],
+                oth.at[j], y_send.at[j], y_recv.at[j], mate,
+            )
+        )
+        e_copies.append(
+            remote(
+                g_ref.at[:, pl.ds(mine + j * piece_width, piece_width)],
+                early.at[j], e_send.at[j], e_recv.at[j], ahead,
+            )
+        )
+        l_copies.append(remote(oth.at[j], late.at[j], l_send.at[j], l_recv.at[j], behind))
+    for j in range(PIECES):
+        y_copies[j].start()
+        e_copies[j].start()
+    flag_copy.start()
+
+    def add(slot, j, left, right, first):
+        lhs = (left[j].astype(jnp.float32) * factor[j]).astype(jnp.bfloat16)
+        product = lax.dot_general(
+            lhs, right[j], (((1,), (1,)), ((), ())), preferred_element_type=jnp.float32
+        )
+        if first:
+            acc[slot] = product
+        else:
+            acc[slot] += product
+
+    def tiles(todo, j, first):
+        @pl.when(y == 0)
+        def _():
+            for slot, left, right in todo:
+                add(slot, j, left, right, first)
+
+        @pl.when(y == 1)
+        def _():
+            for slot, left, right in todo:
+                add(slot, j, right, left, first)
+
+    def over_pieces(todo, arrive):
+        arrive(0)
+        tiles(todo, 0, True)
+
+        def body(j, carry):
+            arrive(j)
+            tiles(todo, j, False)
+            return carry
+
+        lax.fori_loop(1, PIECES, body, 0)
+
+    for copy in own_copies:
+        copy.wait()
+
+    def y_arrive(j):
+        remote(oth.at[j], oth.at[j], y_send.at[j], y_recv.at[j], mate).wait_recv()
+
+    over_pieces([(0, own, oth)], y_arrive)
+    for copy in l_copies:
+        copy.start()
+
+    def e_arrive(j):
+        remote(early.at[j], early.at[j], e_send.at[j], e_recv.at[j], ahead).wait_recv()
+
+    over_pieces([(1, own, early), (2, oth, early)], e_arrive)
+
+    def reduce_and_deliver(slots):
+        low, high = slots[0], len(slots)
+        group = pl.ds(low, high)
+        keep = pl.multiple_of(core * half_rows, 16)
+        give = pl.multiple_of((1 - core) * half_rows, 16)
+        for t in slots:
+            half[t] = acc[t, pl.ds(give, half_rows), :]
+        first = remote(half.at[group], half_in.at[group], h_send.at[low], h_recv.at[low], core_mate)
+        first.start()
+        first.wait_recv()
+        keep_x = pl.multiple_of(x * quarter_rows, 16)
+        give_x = pl.multiple_of((1 - x) * quarter_rows, 16)
+        for t in slots:
+            quarter[t] = acc[t, pl.ds(keep + give_x, quarter_rows), :] + half_in[t, pl.ds(give_x, quarter_rows), :]
+        second = remote(
+            quarter.at[group], quarter_in.at[group], q_send.at[low], q_recv.at[low], x_mate
+        )
+        second.start()
+        for t in slots:
+            piece[t] = acc[t, pl.ds(keep + keep_x, quarter_rows), :] + half_in[t, pl.ds(keep_x, quarter_rows), :]
+        second.wait_recv()
+        for t in slots:
+            piece[t] += quarter_in[t]
+        for t in slots:
+            for i, device in enumerate(owners(t)):
+                here = jnp.logical_and(device[0] == e, device[1] == c)
+                spot = parts.at[y, c]
+
+                @pl.when(here)
+                def _():
+                    pltpu.make_async_copy(piece.at[t], spot, parts_recv.at[y, c]).start()
+
+                @pl.when(jnp.logical_not(here))
+                def _():
+                    remote(piece.at[t], spot, p_send.at[t, i], parts_recv.at[y, c], device).start()
+
+        def finish():
+            first.wait_send()
+            second.wait_send()
+            for t in slots:
+                for i, device in enumerate(owners(t)):
+                    here = jnp.logical_and(device[0] == e, device[1] == c)
+
+                    @pl.when(jnp.logical_not(here))
+                    def _():
+                        remote(
+                            piece.at[t], parts.at[y, c], p_send.at[t, i], parts_recv.at[y, c], device
+                        ).wait_send()
+
+        return finish
+
+    finish_early = reduce_and_deliver((0, 1, 2))
+
+    def l_arrive(j):
+        remote(late.at[j], late.at[j], l_send.at[j], l_recv.at[j], behind).wait_recv()
+
+    over_pieces([(3, late, oth)], l_arrive)
+    finish_late = reduce_and_deliver((3,))
+
+    flag_copy.wait_recv()
+    for row in range(2):
+        for q in range(4):
+            spot = parts.at[row, q]
+            remote(spot, spot, p_send.at[0, 0], parts_recv.at[row, q], mate).wait_recv()
+    for q in range(4):
+        start = (q % 2) * half_rows + (q // 2) * quarter_rows
+        turned[start : start + quarter_rows, :] = parts[0, q] + parts[1, q]
+
+    @pl.when(c < reach)
+    def _():
+        out_ref[...] = turned[...].T * flag_in[0:1, 0:1]
+
+    @pl.when(c >= reach)
+    def _():
+        out_ref[...] = turned[...] * flag_own[0:1, 0:1]
+
+    for j in range(PIECES):
+        y_copies[j].wait_send()
+        e_copies[j].wait_send()
+        l_copies[j].wait_send()
+    flag_copy.wait_send()
+    finish_early()
+    finish_late()
+
+
+def fused(grads, second_moment, step_size, partners, counts):
+    rows, width = grads.shape[1:]
+    reach = partners.shape[1]
+    blocks = lax.axis_size("ex")
+    piece_width = width // 2 // PIECES
+    dma = pltpu.SemaphoreType.DMA
+    vmem = pl.BlockSpec(memory_space=pltpu.VMEM)
+    smem = pl.BlockSpec(memory_space=pltpu.SMEM)
+    gradients = pltpu.VMEM((PIECES, rows, piece_width), jnp.bfloat16)
+    return pl.pallas_call(
+        functools.partial(kernel, blocks, reach),
+        out_shape=jax.ShapeDtypeStruct((rows, rows), jnp.float32),
+        in_specs=[pl.BlockSpec(memory_space=pl.ANY), vmem, smem, smem, smem],
+        out_specs=vmem,
+        scratch_shapes=[
+            gradients, gradients, gradients, gradients,
+            pltpu.VMEM((PIECES, 1, piece_width), jnp.float32),
+            pltpu.VMEM((4, rows, rows), jnp.float32),
+            pltpu.VMEM((4, rows // 2, rows), jnp.float32),
+            pltpu.VMEM((4, rows // 4, rows), jnp.float32),
+            pltpu.VMEM((4, rows // 4, rows), jnp.float32),
+            pltpu.VMEM((4, rows // 2, rows), jnp.float32),
+            pltpu.VMEM((4, rows // 4, rows), jnp.float32),
+            pltpu.VMEM((2, 4, rows // 4, rows), jnp.float32),
+            pltpu.VMEM((8, 128), jnp.float32),
+            pltpu.VMEM((8, 128), jnp.float32),
+            pltpu.VMEM((rows, rows), jnp.float32),
+            dma((PIECES,)), dma((PIECES,)), dma((PIECES,)), dma((PIECES,)), dma((PIECES,)),
+            dma((PIECES,)), dma((PIECES,)),
+            dma((4,)), dma((4,)), dma((4,)), dma((4,)), dma((4, 2)), dma((2, 4)),
+            dma, dma,
+        ],
+        compiler_params=pltpu.CompilerParams(collective_id=0, has_side_effects=True),
+    )(grads[0], second_moment, step_size, partners, counts)
+
+
+def local(grads, second_moment, step_size, partners, counts):
+    rows, width = grads.shape[1:]
+    blocks, ckpts = lax.axis_size("ex"), lax.axis_size("ckpt")
+    fits = partners.shape[1] == 2 and ckpts == 4 and blocks % 2 == 0 and blocks >= 6
+    fits = fits and rows % 64 == 0 and width % (256 * PIECES) == 0
+    body = fused if fits else general
+    return body(grads, second_moment, step_size, partners, counts)
+
+
 def solution(mesh):
     in_specs = (P("ckpt", "ex", None), P("ckpt", None), P("ckpt"), P("ex", None), P("ex"))
     out_specs = P("ex", "ckpt")

time: 184 us -> 88.2 us (0.48)
  waiting for transfers between devices: 147 us -> 0 us
  Pallas kernels: 0 us -> 84.8 us
  between operations: 14.7 us -> 1.3 us
  matrix products: 8.03 us -> 0 us
  starting transfers between devices: 7.27 us -> 0 us
  other arithmetic: 2.96 us -> 0 us
    ppermute x4 -> x0, waiting for transfers between devices: 118 us -> none  [passed_along(): lax.ppermute(value, axis, [(i, (i + by) % length) for i in range(length)])]
    pallas_call x0 -> x1, Pallas kernels: none -> 84.8 us  [fused(): pl.pallas_call(functools.partial(kernel, blocks, reach), out_shape=jax.Sh...]
    unnamed x2 -> x0, waiting for transfers between devices: 29 us -> none
    dot_general x2 -> x0, matrix products: 8.03 us -> none  [local(): lax.dot_general(scaled, visitor, (((0, 2), (0, 2)), ((), ())), preferred_...]
    ppermute x4 -> x0, starting transfers between devices: 7.27 us -> none  [passed_along(): lax.ppermute(value, axis, [(i, (i + by) % length) for i in range(length)])]
  transfers between devices with their start and end apart: 5 -> 0, of which waited for: 4 -> 0; matrix products, arithmetic and copies ran while one was open for 6% -> 0% of each run, Pallas kernels for 0% -> 0%
where the time goes in v1:
time: 88.2 us; the launch traced here: 88 us
  Pallas kernels  84.8 us (96%)
  local copies, waits for them, and re-layouts  1.84 us (2%)
  between operations  1.3 us (1%)
    pallas_call x1, Pallas kernels, fused(): pl.pallas_call(functools.partial(kernel, blocks, reach), out_shape=jax.Sh...  84.8 us
    unnamed x1, local copies, waits for them, and re-layouts  1.84 us

profile of v1, /device:TPU:0, one launch (start us, length us, event | category | flops | bytes accessed | tf_op | source)
XLA Modules:
  0.0 88.0 jit_solution(3277627514510272819)
XLA Ops:
  1.3 84.8 %shard_map.55 = f32[320,320]{1,0:T(8,128)} custom-call(bf16[320,4096]{1,0:T(8,128)(2,1)} %bitcast.1, f32[1,4096]{1,0:T(1,128)} %moment_ref.1, f32[1]{0:T(128)S(6)} %copy.7.step_ref, s32[1,2]{1,0:T(1,128)} %partners_ref.1, s32[1]{0:T(128)S(6)} %copy.8.counts_ref), custom_call_target="tpu_custom_call" | custom-call | tf_op jit(solution)/shard_map/pallas_call | solution.py:285
  86.1 1.8 %copy.9 = f32[320,320]{1,0:T(8,128)} copy(f32[320,320]{1,0:T(8,128)} %shard_map.55) | data formatting | bytes 819200

commit v2 on v1

--- a/solution.py
+++ b/solution.py
@@ -206,11 +206,10 @@
             quarter.at[group], quarter_in.at[group], q_send.at[low], q_recv.at[low], x_mate
         )
         second.start()
-        for t in slots:
-            piece[t] = acc[t, pl.ds(keep + keep_x, quarter_rows), :] + half_in[t, pl.ds(keep_x, quarter_rows), :]
         second.wait_recv()
         for t in slots:
-            piece[t] += quarter_in[t]
+            kept = acc[t, pl.ds(keep + keep_x, quarter_rows), :] + half_in[t, pl.ds(keep_x, quarter_rows), :]
+            piece[t] = (kept + quarter_in[t]).astype(piece.dtype)
         for t in slots:
             for i, device in enumerate(owners(t)):
                 here = jnp.logical_and(device[0] == e, device[1] == c)
@@ -254,7 +253,7 @@
             remote(spot, spot, p_send.at[0, 0], parts_recv.at[row, q], mate).wait_recv()
     for q in range(4):
         start = (q % 2) * half_rows + (q // 2) * quarter_rows
-        turned[start : start + quarter_rows, :] = parts[0, q] + parts[1, q]
+        turned[start : start + quarter_rows, :] = parts[0, q].astype(jnp.float32) + parts[1, q].astype(jnp.float32)
 
     @pl.when(c < reach)
     def _():
@@ -293,10 +292,10 @@
             pltpu.VMEM((4, rows, rows), jnp.float32),
             pltpu.VMEM((4, rows // 2, rows), jnp.float32),
             pltpu.VMEM((4, rows // 4, rows), jnp.float32),
-            pltpu.VMEM((4, rows // 4, rows), jnp.float32),
+            pltpu.VMEM((4, rows // 4, rows), jnp.bfloat16),
             pltpu.VMEM((4, rows // 2, rows), jnp.float32),
             pltpu.VMEM((4, rows // 4, rows), jnp.float32),
-            pltpu.VMEM((2, 4, rows // 4, rows), jnp.float32),
+            pltpu.VMEM((2, 4, rows // 4, rows), jnp.bfloat16),
             pltpu.VMEM((8, 128), jnp.float32),
             pltpu.VMEM((8, 128), jnp.float32),
             pltpu.VMEM((rows, rows), jnp.float32),

time: 88.2 us -> 85.5 us (0.969)
  Pallas kernels: 84.8 us -> 82.1 us
    pallas_call x1, Pallas kernels: 84.8 us -> 82.1 us  [fused(): pl.pallas_call(functools.partial(kernel, blocks, reach), out_shape=jax.Sh...]
where the time goes in v2:
time: 85.5 us; the launch traced here: 85.2 us
  Pallas kernels  82.1 us (96%)
  local copies, waits for them, and re-layouts  1.84 us (2%)
  between operations  1.3 us (2%)
    pallas_call x1, Pallas kernels, fused(): pl.pallas_call(functools.partial(kernel, blocks, reach), out_shape=jax.Sh...  82.1 us
    unnamed x1, local copies, waits for them, and re-layouts  1.84 us

profile of v2, /device:TPU:0, one launch (start us, length us, event | category | flops | bytes accessed | tf_op | source)
XLA Modules:
  0.0 85.2 jit_solution(17372640732953526595)
XLA Ops:
  1.3 82.1 %shard_map.55 = f32[320,320]{1,0:T(8,128)} custom-call(bf16[320,4096]{1,0:T(8,128)(2,1)} %bitcast.1, f32[1,4096]{1,0:T(1,128)} %moment_ref.1, f32[1]{0:T(128)S(6)} %copy.7.step_ref, s32[1,2]{1,0:T(1,128)} %partners_ref.1, s32[1]{0:T(128)S(6)} %copy.8.counts_ref), custom_call_target="tpu_custom_call" | custom-call | tf_op jit(solution)/shard_map/pallas_call | solution.py:284
  83.4 1.8 %copy.9 = f32[320,320]{1,0:T(8,128)} copy(f32[320,320]{1,0:T(8,128)} %shard_map.55) | data formatting | bytes 819200

commit v3 on v2

--- a/solution.py
+++ b/solution.py
@@ -10,6 +10,7 @@
 EPSILON = 1e-08
 MESH = pl.DeviceIdType.MESH
 PIECES = 8
+ROUND_ROWS = 64
 
 
 def passed_along(value, axis, by):
@@ -52,15 +53,17 @@
 def kernel(
     blocks, reach, g_ref, moment_ref, step_ref, partners_ref, counts_ref, out_ref,
     own, oth, early, late, factor, acc, half, quarter, piece, half_in, quarter_in, parts,
-    flag_own, flag_in, turned,
+    flag_own, flag_in, turned, ready, slab, slab_in, late_piece, late_parts, late_sum,
     own_sem, y_send, y_recv, e_send, e_recv, l_send, l_recv,
     h_send, h_recv, q_send, q_recv, p_send, parts_recv, f_send, f_recv,
+    x_send, x_recv, lp_send, late_recv,
 ):
     rows, width = g_ref.shape
     layers = blocks // 2
     span = width // 2
     piece_width = span // PIECES
     half_rows, quarter_rows = rows // 2, rows // 4
+    rounds, share = rows // ROUND_ROWS, ROUND_ROWS // 4
     e = lax.axis_index("ex")
     c = lax.axis_index("ckpt")
     z, y = e // 2, e % 2
@@ -71,6 +74,7 @@
     behind = ((e - 2 * (2 * y - 1) + blocks) % blocks, c)
     core_mate = (e, c + 1 - 2 * core)
     x_mate = (e, (c + 2) % 4)
+    cross_mate = (e, (c + 3 - 2 * core) % 4)
     offset = 2 - ((c + 1) // 2) % 2
     flag_to = ((e + offset) % blocks, c)
     flag_from = ((e - offset + blocks) % blocks, c)
@@ -89,7 +93,7 @@
 
     barrier = pltpu.get_barrier_semaphore()
 
-    for device in [mate, ahead, behind, core_mate, x_mate, flag_from] + sources:
+    for device in [mate, ahead, behind, core_mate, x_mate, cross_mate, flag_from] + sources:
         pl.semaphore_signal(barrier, inc=1, device_id=device, device_id_type=MESH)
 
     mine = pl.multiple_of(y * span, 128)
@@ -113,7 +117,7 @@
     for j in range(PIECES):
         factor[j] = scale[:, j * piece_width : (j + 1) * piece_width]
 
-    pl.semaphore_wait(barrier, 14)
+    pl.semaphore_wait(barrier, 15)
 
     def remote(src, dst, send, recv, device):
         return pltpu.make_async_remote_copy(
@@ -135,7 +139,9 @@
                 early.at[j], e_send.at[j], e_recv.at[j], ahead,
             )
         )
-        l_copies.append(remote(oth.at[j], late.at[j], l_send.at[j], l_recv.at[j], behind))
+    for r in range(rounds):
+        part = oth.at[:, pl.ds(r * ROUND_ROWS, ROUND_ROWS), :]
+        l_copies.append(remote(part, late.at[r], l_send.at[r], l_recv.at[r], behind))
     for j in range(PIECES):
         y_copies[j].start()
         e_copies[j].start()
@@ -240,36 +246,150 @@
 
     finish_early = reduce_and_deliver((0, 1, 2))
 
-    def l_arrive(j):
-        remote(late.at[j], late.at[j], l_send.at[j], l_recv.at[j], behind).wait_recv()
-
-    over_pieces([(3, late, oth)], l_arrive)
-    finish_late = reduce_and_deliver((3,))
+    @pl.when(y == 1)
+    def _():
+        def scale_piece(j, carry):
+            ready[j] = (oth[j].astype(jnp.float32) * factor[j]).astype(jnp.bfloat16)
+            return carry
+
+        lax.fori_loop(0, PIECES, scale_piece, 0)
+
+    def shares(r):
+        out = []
+        for d in range(1, 4):
+            peer = (c + d) % 4
+            given = slab.at[r, pl.ds(pl.multiple_of(peer * share, share), share), :]
+            out.append(
+                remote(given, slab_in.at[r, d - 1], x_send.at[r, d - 1], x_recv.at[r, d - 1], (e, peer))
+            )
+        return out
+
+    def multiply(r):
+        def product(lhs, rhs):
+            return lax.dot_general(
+                lhs, rhs, (((1,), (1,)), ((), ())), preferred_element_type=jnp.float32
+            )
+
+        @pl.when(y == 0)
+        def _():
+            total = jnp.zeros((ROUND_ROWS, rows), jnp.float32)
+            for j in range(PIECES):
+                lhs = (late[r, j].astype(jnp.float32) * factor[j]).astype(jnp.bfloat16)
+                total = total + product(lhs, oth[j])
+            slab[r] = total
+
+        @pl.when(y == 1)
+        def _():
+            total = jnp.zeros((ROUND_ROWS, rows), jnp.float32)
+            for j in range(PIECES):
+                total = total + product(late[r, j], ready[j])
+            slab[r] = total
+
+    late_owners = owners(3)
+
+    def deliver(r):
+        for copy in shares(r):
+            copy.wait_recv()
+        total = slab[r, pl.ds(pl.multiple_of(c * share, share), share), :]
+        for d in range(3):
+            total = total + slab_in[r, d]
+        late_piece[r] = total.astype(late_piece.dtype)
+        for i, device in enumerate(late_owners):
+            here = jnp.logical_and(device[0] == e, device[1] == c)
+            spot = late_parts.at[r, c]
+
+            @pl.when(here)
+            def _():
+                pltpu.make_async_copy(late_piece.at[r], spot, late_recv.at[r, c]).start()
+
+            @pl.when(jnp.logical_not(here))
+            def _():
+                remote(late_piece.at[r], spot, lp_send.at[r, i], late_recv.at[r, c], device).start()
+
+    def one_round(r, carry):
+        remote(late.at[r], late.at[r], l_send.at[r], l_recv.at[r], behind).wait_recv()
+        multiply(r)
+        for copy in shares(r):
+            copy.start()
+
+        @pl.when(r > 0)
+        def _():
+            deliver(r - 1)
+
+        return carry
+
+    lax.fori_loop(0, rounds, one_round, 0)
+    deliver(rounds - 1)
 
     flag_copy.wait_recv()
-    for row in range(2):
+
+    def part_wait(row, q):
+        spot = parts.at[row, q]
+        remote(spot, spot, p_send.at[0, 0], parts_recv.at[row, q], mate).wait_recv()
+
+    def quarter_at(q):
+        start = (q % 2) * half_rows + (q // 2) * quarter_rows
+        return slice(start, start + quarter_rows)
+
+    @pl.when(offset == 1)
+    def _():
         for q in range(4):
-            spot = parts.at[row, q]
-            remote(spot, spot, p_send.at[0, 0], parts_recv.at[row, q], mate).wait_recv()
-    for q in range(4):
-        start = (q % 2) * half_rows + (q // 2) * quarter_rows
-        turned[start : start + quarter_rows, :] = parts[0, q].astype(jnp.float32) + parts[1, q].astype(jnp.float32)
+            part_wait(0, q)
+            part_wait(1, q)
+            both = parts[0, q].astype(jnp.float32) + parts[1, q].astype(jnp.float32)
+            turned[quarter_at(q), :] = both
+
+    @pl.when(offset == 2)
+    def _():
+        for q in range(4):
+            part_wait(odd, q)
+            turned[quarter_at(q), :] = parts[odd, q].astype(jnp.float32)
+        for r in range(rounds):
+            for q in range(4):
+                spot = late_parts.at[r, q]
+                remote(spot, spot, lp_send.at[0, 0], late_recv.at[r, q], mate).wait_recv()
+                start = r * ROUND_ROWS + q * share
+                late_sum[start : start + share, :] = late_parts[r, q].astype(jnp.float32)
+
+    @pl.when(jnp.logical_and(offset == 2, odd == 1))
+    def _():
+        turned[...] += late_sum[...]
+
+    flipped = jnp.logical_and(offset == 2, odd == 0)
 
     @pl.when(c < reach)
     def _():
         out_ref[...] = turned[...].T * flag_in[0:1, 0:1]
 
+        @pl.when(flipped)
+        def _():
+            out_ref[...] += late_sum[...] * flag_in[0:1, 0:1]
+
     @pl.when(c >= reach)
     def _():
         out_ref[...] = turned[...] * flag_own[0:1, 0:1]
+
+        @pl.when(flipped)
+        def _():
+            out_ref[...] += late_sum[...].T * flag_own[0:1, 0:1]
 
     for j in range(PIECES):
         y_copies[j].wait_send()
         e_copies[j].wait_send()
-        l_copies[j].wait_send()
     flag_copy.wait_send()
     finish_early()
-    finish_late()
+    for r in range(rounds):
+        l_copies[r].wait_send()
+        for copy in shares(r):
+            copy.wait_send()
+        for i, device in enumerate(late_owners):
+            here = jnp.logical_and(device[0] == e, device[1] == c)
+
+            @pl.when(jnp.logical_not(here))
+            def _():
+                remote(
+                    late_piece.at[r], late_parts.at[r, c], lp_send.at[r, i], late_recv.at[r, c], device
+                ).wait_send()
 
 
 def fused(grads, second_moment, step_size, partners, counts):
@@ -280,6 +400,7 @@
     dma = pltpu.SemaphoreType.DMA
     vmem = pl.BlockSpec(memory_space=pltpu.VMEM)
     smem = pl.BlockSpec(memory_space=pltpu.SMEM)
+    rounds, share = rows // ROUND_ROWS, ROUND_ROWS // 4
     gradients = pltpu.VMEM((PIECES, rows, piece_width), jnp.bfloat16)
     return pl.pallas_call(
         functools.partial(kernel, blocks, reach),
@@ -287,9 +408,10 @@
         in_specs=[pl.BlockSpec(memory_space=pl.ANY), vmem, smem, smem, smem],
         out_specs=vmem,
         scratch_shapes=[
-            gradients, gradients, gradients, gradients,
+            gradients, gradients, gradients,
+            pltpu.VMEM((rounds, PIECES, ROUND_ROWS, piece_width), jnp.bfloat16),
             pltpu.VMEM((PIECES, 1, piece_width), jnp.float32),
-            pltpu.VMEM((4, rows, rows), jnp.float32),
+            pltpu.VMEM((3, rows, rows), jnp.float32),
             pltpu.VMEM((4, rows // 2, rows), jnp.float32),
             pltpu.VMEM((4, rows // 4, rows), jnp.float32),
             pltpu.VMEM((4, rows // 4, rows), jnp.bfloat16),
@@ -299,10 +421,17 @@
             pltpu.VMEM((8, 128), jnp.float32),
             pltpu.VMEM((8, 128), jnp.float32),
             pltpu.VMEM((rows, rows), jnp.float32),
+            gradients,
+            pltpu.VMEM((rounds, ROUND_ROWS, rows), jnp.float32),
+            pltpu.VMEM((rounds, 3, share, rows), jnp.float32),
+            pltpu.VMEM((rounds, share, rows), jnp.bfloat16),
+            pltpu.VMEM((rounds, 4, share, rows), jnp.bfloat16),
+            pltpu.VMEM((rows, rows), jnp.float32),
             dma((PIECES,)), dma((PIECES,)), dma((PIECES,)), dma((PIECES,)), dma((PIECES,)),
-            dma((PIECES,)), dma((PIECES,)),
+            dma((rounds,)), dma((rounds,)),
             dma((4,)), dma((4,)), dma((4,)), dma((4,)), dma((4, 2)), dma((2, 4)),
             dma, dma,
+            dma((rounds, 3)), dma((rounds, 3)), dma((rounds, 2)), dma((rounds, 4)),
         ],
         compiler_params=pltpu.CompilerParams(collective_id=0, has_side_effects=True),
     )(grads[0], second_moment, step_size, partners, counts)

time: 85.5 us -> 83.3 us (0.974)
  Pallas kernels: 82.1 us -> 79.8 us
    pallas_call x1, Pallas kernels: 82.1 us -> 79.8 us  [fused(): pl.pallas_call(functools.partial(kernel, blocks, reach), out_shape=jax.Sh...]
where the time goes in v3:
time: 83.3 us; the launch traced here: 83 us
  Pallas kernels  79.8 us (96%)
  local copies, waits for them, and re-layouts  1.84 us (2%)
  between operations  1.3 us (2%)
    pallas_call x1, Pallas kernels, fused(): pl.pallas_call(functools.partial(kernel, blocks, reach), out_shape=jax.Sh...  79.8 us
    unnamed x1, local copies, waits for them, and re-layouts  1.84 us

profile of v3, /device:TPU:0, one launch (start us, length us, event | category | flops | bytes accessed | tf_op | source)
XLA Modules:
  0.0 83.0 jit_solution(1585902780540991688)
XLA Ops:
  1.3 79.8 %shard_map.55 = f32[320,320]{1,0:T(8,128)} custom-call(bf16[320,4096]{1,0:T(8,128)(2,1)} %bitcast.1, f32[1,4096]{1,0:T(1,128)} %moment_ref.1, f32[1]{0:T(128)S(6)} %copy.7.step_ref, s32[1,2]{1,0:T(1,128)} %partners_ref.1, s32[1]{0:T(128)S(6)} %copy.8.counts_ref), custom_call_target="tpu_custom_call" | custom-call | tf_op jit(solution)/shard_map/pallas_call | solution.py:405
  81.2 1.8 %copy.9 = f32[320,320]{1,0:T(8,128)} copy(f32[320,320]{1,0:T(8,128)} %shard_map.55) | data formatting | bytes 819200

commit v4 on v3

--- a/solution.py
+++ b/solution.py
@@ -53,10 +53,10 @@
 def kernel(
     blocks, reach, g_ref, moment_ref, step_ref, partners_ref, counts_ref, out_ref,
     own, oth, early, late, factor, acc, half, quarter, piece, half_in, quarter_in, parts,
-    flag_own, flag_in, turned, ready, slab, slab_in, late_piece, late_parts, late_sum,
+    flag_own, flag_in, turned, ready, slab, slab_in, late_piece, late_parts, extra,
     own_sem, y_send, y_recv, e_send, e_recv, l_send, l_recv,
     h_send, h_recv, q_send, q_recv, p_send, parts_recv, f_send, f_recv,
-    x_send, x_recv, lp_send, late_recv,
+    x_send, x_recv, lp_send, late_recv, t_send, t_recv,
 ):
     rows, width = g_ref.shape
     layers = blocks // 2
@@ -80,7 +80,7 @@
     flag_from = ((e - offset + blocks) % blocks, c)
 
     def owners(slot):
-        a, o = [(2 * z, 1), (2 * z - y, 2), (2 * z + 1 - 2 * y, 1), (2 * z - 1 + y, 2)][slot]
+        a, o = [(2 * z, 1), (2 * z + 1 - 2 * y, 1), (2 * z - y, 2), (2 * z - 1 + y, 2)][slot]
         a = (a + blocks) % blocks
         return (a, reach - 1 + o), ((a + o) % blocks, reach - o)
 
@@ -147,10 +147,12 @@
         e_copies[j].start()
     flag_copy.start()
 
-    def add(slot, j, left, right, first):
-        lhs = (left[j].astype(jnp.float32) * factor[j]).astype(jnp.bfloat16)
+    def scaled(ref, j):
+        return (ref[j].astype(jnp.float32) * factor[j]).astype(jnp.bfloat16)
+
+    def add(slot, lhs, rhs, first):
         product = lax.dot_general(
-            lhs, right[j], (((1,), (1,)), ((), ())), preferred_element_type=jnp.float32
+            lhs, rhs, (((1,), (1,)), ((), ())), preferred_element_type=jnp.float32
         )
         if first:
             acc[slot] = product
@@ -161,12 +163,15 @@
         @pl.when(y == 0)
         def _():
             for slot, left, right in todo:
-                add(slot, j, left, right, first)
+                if slot == 2:
+                    add(slot, right[j], scaled(left, j), first)
+                else:
+                    add(slot, scaled(left, j), right[j], first)
 
         @pl.when(y == 1)
         def _():
             for slot, left, right in todo:
-                add(slot, j, right, left, first)
+                add(slot, scaled(right, j), left[j], first)
 
     def over_pieces(todo, arrive):
         arrive(0)
@@ -192,7 +197,13 @@
     def e_arrive(j):
         remote(early.at[j], early.at[j], e_send.at[j], e_recv.at[j], ahead).wait_recv()
 
-    over_pieces([(1, own, early), (2, oth, early)], e_arrive)
+    over_pieces([(2, own, early), (1, oth, early)], e_arrive)
+    extra_copies = []
+    for r in range(rounds):
+        part = pl.ds(r * ROUND_ROWS, ROUND_ROWS)
+        extra_copies.append(remote(acc.at[2, part, :], extra.at[r], t_send.at[r], t_recv.at[r], mate))
+    for copy in extra_copies:
+        copy.start()
 
     def reduce_and_deliver(slots):
         low, high = slots[0], len(slots)
@@ -201,7 +212,7 @@
         give = pl.multiple_of((1 - core) * half_rows, 16)
         for t in slots:
             half[t] = acc[t, pl.ds(give, half_rows), :]
-        first = remote(half.at[group], half_in.at[group], h_send.at[low], h_recv.at[low], core_mate)
+        first = remote(half.at[group], half_in.at[group], h_send, h_recv, core_mate)
         first.start()
         first.wait_recv()
         keep_x = pl.multiple_of(x * quarter_rows, 16)
@@ -209,7 +220,7 @@
         for t in slots:
             quarter[t] = acc[t, pl.ds(keep + give_x, quarter_rows), :] + half_in[t, pl.ds(give_x, quarter_rows), :]
         second = remote(
-            quarter.at[group], quarter_in.at[group], q_send.at[low], q_recv.at[low], x_mate
+            quarter.at[group], quarter_in.at[group], q_send, q_recv, x_mate
         )
         second.start()
         second.wait_recv()
@@ -244,7 +255,7 @@
 
         return finish
 
-    finish_early = reduce_and_deliver((0, 1, 2))
+    finish_early = reduce_and_deliver((0, 1))
 
     @pl.when(y == 1)
     def _():
@@ -276,14 +287,14 @@
             for j in range(PIECES):
                 lhs = (late[r, j].astype(jnp.float32) * factor[j]).astype(jnp.bfloat16)
                 total = total + product(lhs, oth[j])
-            slab[r] = total
+            slab[r] = total + extra[r]
 
         @pl.when(y == 1)
         def _():
             total = jnp.zeros((ROUND_ROWS, rows), jnp.float32)
             for j in range(PIECES):
                 total = total + product(late[r, j], ready[j])
-            slab[r] = total
+            slab[r] = total + extra[r]
 
     late_owners = owners(3)
 
@@ -308,6 +319,7 @@
 
     def one_round(r, carry):
         remote(late.at[r], late.at[r], l_send.at[r], l_recv.at[r], behind).wait_recv()
+        remote(extra.at[r], extra.at[r], t_send.at[r], t_recv.at[r], mate).wait_recv()
         multiply(r)
         for copy in shares(r):
             copy.start()
@@ -341,37 +353,23 @@
 
     @pl.when(offset == 2)
     def _():
-        for q in range(4):
-            part_wait(odd, q)
-            turned[quarter_at(q), :] = parts[odd, q].astype(jnp.float32)
         for r in range(rounds):
             for q in range(4):
                 spot = late_parts.at[r, q]
                 remote(spot, spot, lp_send.at[0, 0], late_recv.at[r, q], mate).wait_recv()
                 start = r * ROUND_ROWS + q * share
-                late_sum[start : start + share, :] = late_parts[r, q].astype(jnp.float32)
-
-    @pl.when(jnp.logical_and(offset == 2, odd == 1))
+                turned[start : start + share, :] = late_parts[r, q].astype(jnp.float32)
+
+    turn = (1 - x + (offset - 1) * (1 - odd)) % 2
+    listed = flag_own[0:1, 0:1] * x.astype(jnp.float32) + flag_in[0:1, 0:1] * (1 - x).astype(jnp.float32)
+
+    @pl.when(turn == 1)
     def _():
-        turned[...] += late_sum[...]
-
-    flipped = jnp.logical_and(offset == 2, odd == 0)
-
-    @pl.when(c < reach)
+        out_ref[...] = turned[...].T * listed
+
+    @pl.when(turn == 0)
     def _():
-        out_ref[...] = turned[...].T * flag_in[0:1, 0:1]
-
-        @pl.when(flipped)
-        def _():
-            out_ref[...] += late_sum[...] * flag_in[0:1, 0:1]
-
-    @pl.when(c >= reach)
-    def _():
-        out_ref[...] = turned[...] * flag_own[0:1, 0:1]
-
-        @pl.when(flipped)
-        def _():
-            out_ref[...] += late_sum[...].T * flag_own[0:1, 0:1]
+        out_ref[...] = turned[...] * listed
 
     for j in range(PIECES):
         y_copies[j].wait_send()
@@ -380,6 +378,7 @@
     finish_early()
     for r in range(rounds):
         l_copies[r].wait_send()
+        extra_copies[r].wait_send()
         for copy in shares(r):
             copy.wait_send()
         for i, device in enumerate(late_owners):
@@ -412,11 +411,11 @@
             pltpu.VMEM((rounds, PIECES, ROUND_ROWS, piece_width), jnp.bfloat16),
             pltpu.VMEM((PIECES, 1, piece_width), jnp.float32),
             pltpu.VMEM((3, rows, rows), jnp.float32),
-            pltpu.VMEM((4, rows // 2, rows), jnp.float32),
-            pltpu.VMEM((4, rows // 4, rows), jnp.float32),
-            pltpu.VMEM((4, rows // 4, rows), jnp.bfloat16),
-            pltpu.VMEM((4, rows // 2, rows), jnp.float32),
-            pltpu.VMEM((4, rows // 4, rows), jnp.float32),
+            pltpu.VMEM((2, rows // 2, rows), jnp.float32),
+            pltpu.VMEM((2, rows // 4, rows), jnp.float32),
+            pltpu.VMEM((2, rows // 4, rows), jnp.bfloat16),
+            pltpu.VMEM((2, rows // 2, rows), jnp.float32),
+            pltpu.VMEM((2, rows // 4, rows), jnp.float32),
             pltpu.VMEM((2, 4, rows // 4, rows), jnp.bfloat16),
             pltpu.VMEM((8, 128), jnp.float32),
             pltpu.VMEM((8, 128), jnp.float32),
@@ -426,12 +425,13 @@
             pltpu.VMEM((rounds, 3, share, rows), jnp.float32),
             pltpu.VMEM((rounds, share, rows), jnp.bfloat16),
             pltpu.VMEM((rounds, 4, share, rows), jnp.bfloat16),
-            pltpu.VMEM((rows, rows), jnp.float32),
+            pltpu.VMEM((rounds, ROUND_ROWS, rows), jnp.float32),
             dma((PIECES,)), dma((PIECES,)), dma((PIECES,)), dma((PIECES,)), dma((PIECES,)),
             dma((rounds,)), dma((rounds,)),
-            dma((4,)), dma((4,)), dma((4,)), dma((4,)), dma((4, 2)), dma((2, 4)),
+            dma, dma, dma, dma, dma((2, 2)), dma((2, 4)),
             dma, dma,
             dma((rounds, 3)), dma((rounds, 3)), dma((rounds, 2)), dma((rounds, 4)),
+            dma((rounds,)), dma((rounds,)),
         ],
         compiler_params=pltpu.CompilerParams(collective_id=0, has_side_effects=True),
     )(grads[0], second_moment, step_size, partners, counts)

time: 83.3 us -> 82.9 us (level)
  no operation moved by 1% of the time
where the time goes in v4:
time: 82.9 us; the launch traced here: 82.6 us
  Pallas kernels  79.5 us (96%)
  local copies, waits for them, and re-layouts  1.84 us (2%)
  between operations  1.3 us (2%)
    pallas_call x1, Pallas kernels, fused(): pl.pallas_call(functools.partial(kernel, blocks, reach), out_shape=jax.Sh...  79.5 us
    unnamed x1, local copies, waits for them, and re-layouts  1.84 us

profile of v4, /device:TPU:0, one launch (start us, length us, event | category | flops | bytes accessed | tf_op | source)
XLA Modules:
  0.0 82.6 jit_solution(13546540805420917041)
XLA Ops:
  1.3 79.5 %shard_map.55 = f32[320,320]{1,0:T(8,128)} custom-call(bf16[320,4096]{1,0:T(8,128)(2,1)} %bitcast.1, f32[1,4096]{1,0:T(1,128)} %moment_ref.1, f32[1]{0:T(128)S(6)} %copy.7.step_ref, s32[1,2]{1,0:T(1,128)} %partners_ref.1, s32[1]{0:T(128)S(6)} %copy.8.counts_ref), custom_call_target="tpu_custom_call" | custom-call | tf_op jit(solution)/shard_map/pallas_call | solution.py:404
  80.8 1.8 %copy.9 = f32[320,320]{1,0:T(8,128)} copy(f32[320,320]{1,0:T(8,128)} %shard_map.55) | data formatting | bytes 819200

commit v5 on v4

--- a/solution.py
+++ b/solution.py
@@ -9,7 +9,7 @@
 
 EPSILON = 1e-08
 MESH = pl.DeviceIdType.MESH
-PIECES = 8
+PIECES = 4
 ROUND_ROWS = 64
 
 
@@ -190,9 +190,14 @@
     def y_arrive(j):
         remote(oth.at[j], oth.at[j], y_send.at[j], y_recv.at[j], mate).wait_recv()
 
-    over_pieces([(0, own, oth)], y_arrive)
+    def wait_piece(j, carry):
+        y_arrive(j)
+        return carry
+
+    lax.fori_loop(0, PIECES, wait_piece, 0)
     for copy in l_copies:
         copy.start()
+    over_pieces([(0, own, oth)], lambda j: None)
 
     def e_arrive(j):
         remote(early.at[j], early.at[j], e_send.at[j], e_recv.at[j], ahead).wait_recv()

time: 82.9 us -> 82.4 us (level)
  no operation moved by 1% of the time
where the time goes in v5:
time: 82.4 us; the launch traced here: 82.1 us
  Pallas kernels  79 us (96%)
  local copies, waits for them, and re-layouts  1.84 us (2%)
  between operations  1.3 us (2%)
    pallas_call x1, Pallas kernels, fused(): pl.pallas_call(functools.partial(kernel, blocks, reach), out_shape=jax.Sh...  79 us
    unnamed x1, local copies, waits for them, and re-layouts  1.84 us

profile of v5, /device:TPU:0, one launch (start us, length us, event | category | flops | bytes accessed | tf_op | source)
XLA Modules:
  0.0 82.1 jit_solution(10554751722050579235)
XLA Ops:
  1.3 79.0 %shard_map.55 = f32[320,320]{1,0:T(8,128)} custom-call(bf16[320,4096]{1,0:T(8,128)(2,1)} %bitcast.1, f32[1,4096]{1,0:T(1,128)} %moment_ref.1, f32[1]{0:T(128)S(6)} %copy.7.step_ref, s32[1,2]{1,0:T(1,128)} %partners_ref.1, s32[1]{0:T(128)S(6)} %copy.8.counts_ref), custom_call_target="tpu_custom_call" | custom-call | tf_op jit(solution)/shard_map/pallas_call | solution.py:409
  80.3 1.8 %copy.9 = f32[320,320]{1,0:T(8,128)} copy(f32[320,320]{1,0:T(8,128)} %shard_map.55) | data formatting | bytes 819200
